TPU v7x, 32 devices: a whole 2x2x4 slice. The times are simulated.
32 devices in a mesh: dp: 8 (over y, x, core), expert: 4 (over z).
Axes of the slice: x: 2, y: 2, z: 4, core: 2. Of those that a mesh axis runs over, the one named last changes fastest.
Arguments:
- grad_out: bfloat16 [4096, 2048], P(('dp', 'expert')), may hold values from -6 to 6
- probs: bfloat16 [4096, 2], P(('dp', 'expert')), may hold values from 0.099609375 to 1
- routes: int32 [4096, 2], P(('dp', 'expert')), may hold values from 0 to 3, all different within a row; in each aligned block of 128 rows (0 to 127, 128 to 255, ...) at most 80 rows name the same one
- hidden: bfloat16 [4, 2560, 7168], P('expert', None, 'dp'), may hold values from -0.119628906 to 0.119628906
- w_down: bfloat16 [4, 7168, 2048], P('expert', 'dp'), may hold values from -0.125 to 0.125
Outputs:
- grad_hidden: bfloat16 [4, 2560, 7168], P('expert', None, 'dp')
- grad_down: bfloat16 [4, 7168, 2048], P('expert', 'dp')
- grad_probs: float32 [4096, 2], P(('dp', 'expert'))
Inputs may be any that keep to these rules, and one draw needn't show every extreme that they name: Within the 128 tokens of one device no expert is named by more than 80 routes; the 2 routes of a token name different experts; every expert is named somewhere.
All inputs are finite; a program needn't handle non-finite values.
Results may differ from a plain program's by a relative error of at most 0.0049.
Values may be sent and summed in bfloat16 or wider, within the bound.
A program may use at most 128 MiB of HBM per device.

v0:
```python
import jax
import jax.numpy as jnp
from jax import lax
from jax.sharding import PartitionSpec as P


def on_device(grad_out, probs, routes, hidden, w_down):
    expert_count = lax.axis_size("expert")
    token_count = routes.shape[0]
    route_width = routes.shape[1]
    capacity = token_count * route_width * 5 // (4 * expert_count)
    flattened = routes.reshape(-1)
    expert_ids = jnp.arange(expert_count, dtype=jnp.int32)
    one_hot = (flattened[:, None] == expert_ids[None, :]).astype(jnp.int32)
    ranking = jnp.cumsum(one_hot, axis=0) - 1
    destination = (flattened * capacity + jnp.sum(one_hot * ranking, axis=1)).reshape(
        token_count, route_width
    )
    places = jnp.arange(expert_count * capacity, dtype=jnp.int32)
    matches = destination[None, :, :] == places[:, None, None]
    selector = jnp.any(matches, axis=2).astype(jnp.bfloat16)
    sent_rows = jnp.dot(selector, grad_out, preferred_element_type=jnp.float32).astype(jnp.bfloat16)
    sent_probs = jnp.sum(
        jnp.where(matches, probs.astype(jnp.float32)[None, :, :], 0.0), axis=(1, 2)
    ).astype(jnp.bfloat16)
    width = grad_out.shape[1]
    recv_rows, recv_probs = (
        lax.all_to_all(
            sent_rows.reshape(expert_count, capacity, width),
            "expert",
            split_axis=0,
            concat_axis=0,
            tiled=True,
        ),
        lax.all_to_all(
            sent_probs.reshape(expert_count, capacity),
            "expert",
            split_axis=0,
            concat_axis=0,
            tiled=True,
        ),
    )
    block_rows = recv_rows.reshape(expert_count * capacity, width)
    block_probs = recv_probs.reshape(expert_count * capacity)
    saved = hidden[0]
    weights = w_down[0]
    all_rows, all_probs = (
        lax.all_gather(block_rows, "dp", axis=0, tiled=True),
        lax.all_gather(block_probs, "dp", axis=0, tiled=True),
    )
    weight_col = all_probs.astype(jnp.float32)[:, None]
    scaled = (weight_col * all_rows.astype(jnp.float32)).astype(jnp.bfloat16)
    back_hidden = lax.dot_general(
        all_rows, weights, (((1,), (1,)), ((), ())), preferred_element_type=jnp.float32
    )
    grad_rows = (weight_col * back_hidden).astype(jnp.bfloat16)
    slot_probs = jnp.sum(saved.astype(jnp.float32) * back_hidden, axis=1)
    grad_weight = lax.dot_general(
        saved, scaled, (((0,), (0,)), ((), ())), preferred_element_type=jnp.float32
    )
    grad_rows, slot_probs, grad_weight = (grad_rows, slot_probs, grad_weight)
    own_probs = lax.psum_scatter(slot_probs, "dp", scatter_dimension=0, tiled=True)
    back_probs = lax.all_to_all(
        own_probs.reshape(expert_count, capacity), "expert", split_axis=0, concat_axis=0, tiled=True
    )
    grad_probs = jnp.sum(jnp.where(matches, back_probs.reshape(-1)[:, None, None], 0.0), axis=0)
    return (grad_rows[None], grad_weight.astype(jnp.bfloat16)[None], grad_probs)


def solution(mesh):
    in_specs = (
        P(("dp", "expert"), None),
        P(("dp", "expert"), None),
        P(("dp", "expert"), None),
        P("expert", None, "dp"),
        P("expert", "dp", None),
    )
    out_specs = (P("expert", None, "dp"), P("expert", "dp", None), P(("dp", "expert"), None))
    return jax.shard_map(
        on_device, mesh=mesh, in_specs=in_specs, out_specs=out_specs, check_vma=False
    )
```

profile of v0, /device:TPU:0, one launch (start us, length us, event | category | flops | bytes accessed | tf_op | source)
XLA Modules:
  0.0 229.8 jit_solution(13012284023979416123)
XLA Ops:
  7.2 0.0 copy-start
  7.2 0.0 all-gather.2.cloned.1.call-start
  7.2 0.8 copy.47
  8.1 0.1 eq.42
  8.2 0.1 eq.38
  8.4 1.2 reduce-window.6
  9.6 0.1 slice.8
  9.7 0.1 copy.49
  9.8 0.1 copy.50
  9.9 0.1 add_bitcast_fusion
  10.0 0.1 reduce_sum.39
  10.1 0.1 copy.51
  10.2 0.7 multiply_add_fusion
  11.0 0.0 copy-done
  11.0 0.5 convolution_convert_fusion
  11.5 37.6 %all_to_all.20 = bf16[4,80,2048]{2,1,0:T(8,128)(2,1)} all-to-all(bf16[4,80,2048]{2,1,0:T(8,128)(2,1)S(1)} %bitcast.41), channel_id=1, replica_groups=mesh['dp'=8,'expert'=4] {'expert'}, dimensions={0} | all-to-all | bytes 2621440 | tf_op jit(solution)/shard_map/all_to_all | solution.py:28
  49.1 0.0 all-gather.2.cloned.1.call-update
  49.1 0.0 copy-start.1
  49.1 7.4 %copy.53 = bf16[1,2560,896]{1,2,0:T(8,128)(2,1)} copy(bf16[1,2560,896]{2,1,0:T(8,128)(2,1)} %param.8) | data formatting | bytes 9175040 | tf_op args[3]
  56.5 0.0 copy-done.1
  56.5 0.6 fusion.11
  57.7 0.0 copy-start.2
  57.7 53.8 %all-gather.2.cloned.1.call-done = bf16[2560,2048]{1,0:T(8,128)(2,1)} async-done(((bf16[320,2048]{1,0:T(8,128)(2,1)}), bf16[2560,2048]{1,0:T(8,128)(2,1)}) %all-gather.2.cloned.1.call-update) | async-done | bytes 10485776 | tf_op jit(solution)/shard_map/all_gather | solution.py:48
  111.5 16.4 %multiply_reduce_fusion = (f32[2560]{0:T(1024)S(1)}, f32[2560,896]{0,1:T(8,128)}) fusion(bf16[1,2560,896]{1,2,0:T(8,128)(2,1)} %copy.53, bf16[2560,2048]{1,0:T(8,128)(2,1)} %all-gather.2.cloned.1.call-done, bf16[1,896,2048]{2,1,0:T(8,128)(2,1)} %param.9), kind=kOutput, calls=%fused_computation.3 | convolution fusion | flops 9402120192 | bytes 27928576 | tf_op jit(solution)/shard_map/dot_general | solution.py:53
  127.9 23.5 %all-reduce.1 = f32[2560]{0:T(1024)S(1)} all-reduce(f32[2560]{0:T(1024)S(1)} %get-tuple-element.22), channel_id=2, replica_groups=mesh['dp'=8,'expert'=4] {'dp'}, use_global_device_ids=true, to_apply=%region_6.7.clone | all-reduce | flops 2560 | bytes 20480
  151.4 0.1 dynamic-slice.2
  151.4 0.7 all_to_all.15
  152.1 4.6 %all-to-all-start.2 = ((f32[4,1,80]{2,1,0:T(1,128)}), f32[4,1,80]{2,1,0:T(1,128)S(1)}, u32[]{:S(2)}, u32[]{:S(2)}) async-start(f32[4,1,80]{2,1,0:T(1,128)} %all_to_all.15), calls=%async_computation.2 | async-start | bytes 4096 | tf_op jit(solution)/shard_map/all_to_all | solution.py:63
  156.7 0.0 copy-done.2
  156.7 5.5 %all-to-all-done.2 = f32[4,1,80]{2,1,0:T(1,128)S(1)} async-done(((f32[4,1,80]{2,1,0:T(1,128)}), f32[4,1,80]{2,1,0:T(1,128)S(1)}, u32[]{:S(2)}, u32[]{:S(2)}) %all-to-all-start.2) | async-done | bytes 1312 | tf_op jit(solution)/shard_map/all_to_all | solution.py:63
  162.2 0.5 broadcast.37
  162.7 0.7 reduce.4
  163.4 0.1 broadcast_in_dim.38
  163.5 0.7 select_reduce_fusion
  164.2 0.7 convert_element_type.59
  164.8 3.2 %all-to-all-start = ((bf16[4,1,80]{2,1,0:T(2,128)(2,1)}), bf16[4,1,80]{2,1,0:T(2,128)(2,1)S(1)}, u32[]{:S(2)}, u32[]{:S(2)}) async-start(bf16[4,1,80]{2,1,0:T(2,128)(2,1)} %convert_element_type.59), calls=%async_computation | async-start | bytes 4096 | tf_op jit(solution)/shard_map/all_to_all | solution.py:35
  168.6 4.9 %all-to-all-done = bf16[4,1,80]{2,1,0:T(2,128)(2,1)S(1)} async-done(((bf16[4,1,80]{2,1,0:T(2,128)(2,1)}), bf16[4,1,80]{2,1,0:T(2,128)(2,1)S(1)}, u32[]{:S(2)}, u32[]{:S(2)}) %all-to-all-start) | async-done | bytes 672 | tf_op jit(solution)/shard_map/all_to_all | solution.py:35
  173.5 0.1 reshape.69
  173.6 0.2 dynamic-update-slice
  173.9 12.2 %all-reduce = bf16[2560]{0:T(1024)(128)(2,1)S(1)} all-reduce(bf16[2560]{0:T(1024)(128)(2,1)S(1)} %dynamic-update-slice), channel_id=1, replica_groups=mesh['dp'=8,'expert'=4] {'dp'}, use_global_device_ids=true, to_apply=%add | all-reduce | flops 2560 | bytes 10240
  186.1 6.8 %fusion.2 = bf16[1,2560,896]{1,2,0:T(8,128)(2,1)} fusion(f32[2560,896]{0,1:T(8,128)} %get-tuple-element.23, f32[2560]{0:T(1024)S(1)} %convert_element_type.51), kind=kLoop, calls=%fused_computation.5 | loop fusion | flops 4587520 | bytes 13772800 | tf_op jit(solution)/shard_map/broadcast_in_dim | solution.py:67
  192.9 7.2 %copy.54 = bf16[1,2560,896]{2,1,0:T(8,128)(2,1)} copy(bf16[1,2560,896]{1,2,0:T(8,128)(2,1)} %fusion.2) | data formatting | bytes 9175040
  200.1 16.8 %convert_bitcast_fusion = bf16[1,896,2048]{1,2,0:T(8,128)(2,1)} fusion(bf16[1,2560,896]{2,1,0:T(8,128)(2,1)} %param.8, bf16[2560,2048]{1,0:T(8,128)(2,1)} %all-gather.2.cloned.1.call-done, f32[2560]{0:T(1024)S(1)} %convert_element_type.51), kind=kOutput, calls=%fused_computation.9 | convolution fusion | flops 9412804608 | bytes 18753536 | tf_op jit(solution)/shard_map/dot_general | solution.py:58
  216.9 6.0 %copy.55 = bf16[1,896,2048]{2,1,0:T(8,128)(2,1)} copy(bf16[1,896,2048]{1,2,0:T(8,128)(2,1)} %convert_bitcast_fusion) | data formatting | bytes 7340032
  (9 shorter events, 0.1 us)
Async XLA Ops:
  7.2 3.8 %copy-start = (bf16[128,2048]{1,0:T(8,128)(2,1)S(1)}, bf16[128,2048]{1,0:T(8,128)(2,1)}, u32[]{:S(2)}) copy-start(bf16[128,2048]{1,0:T(8,128)(2,1)} %param.5) | copy-start | bytes 1572868
  7.2 104.3 %all-gather.2.cloned.1.call-start = ((), (), s32[]{:S(2)}) async-start(), calls=%async_computation.3 | async-start | bytes 11796480 | tf_op jit(solution)/shard_map/all_gather | solution.py:48
  49.1 7.4 %copy-start.1 = (u32[32]{0:T(128)S(1)}, u32[32]{0:T(128)}, u32[]{:S(2)}) copy-start(u32[32]{0:T(128)} %constant.19) | copy-start | bytes 388
  57.7 99.0 %copy-start.2 = (bf16[128,2]{0,1:T(2,128)(2,1)S(1)}, bf16[128,2]{0,1:T(2,128)(2,1)}, u32[]{:S(2)}) copy-start(bf16[128,2]{0,1:T(2,128)(2,1)} %param.6) | copy-start | bytes 1540
  152.1 10.1 %all-to-all-start.2 = ((f32[4,1,80]{2,1,0:T(1,128)}), f32[4,1,80]{2,1,0:T(1,128)S(1)}, u32[]{:S(2)}, u32[]{:S(2)}) async-start(f32[4,1,80]{2,1,0:T(1,128)} %all_to_all.15), calls=%async_computation.2 | async-start | bytes 4096 | tf_op jit(solution)/shard_map/all_to_all | solution.py:63
  164.8 8.7 %all-to-all-start = ((bf16[4,1,80]{2,1,0:T(2,128)(2,1)}), bf16[4,1,80]{2,1,0:T(2,128)(2,1)S(1)}, u32[]{:S(2)}, u32[]{:S(2)}) async-start(bf16[4,1,80]{2,1,0:T(2,128)(2,1)} %convert_element_type.59), calls=%async_computation | async-start | bytes 4096 | tf_op jit(solution)/shard_map/all_to_all | solution.py:35
Sparse Core Ops, SparseCore 0:
  49.2 62.2 all-gather.1
where the time goes:
time: 231 us; the launch traced here: 230 us
  blocking collectives  73.3 us (32%)
  waiting for transfers between devices  64.2 us (28%)
  matrix products  33.7 us (15%)
  local copies, waits for them, and re-layouts  25.1 us (11%)
  between operations  15.4 us (7%)
  other arithmetic  10.3 us (4%)
  starting transfers between devices  7.86 us (3%)
    all_gather x1, waiting for transfers between devices, on_device(): lax.all_gather(block_rows, 'dp', axis=0, tiled=True)  53.8 us
    all_to_all x1, blocking collectives, on_device(): lax.all_to_all(sent_rows.reshape(expert_count, capacity, width), 'expert'...  37.6 us
    unnamed x2, blocking collectives  35.7 us
    unnamed x14, local copies, waits for them, and re-layouts  22.3 us
    dot_general x1, matrix products, on_device(): lax.dot_general(saved, scaled, (((0,), (0,)), ((), ())), preferred_elemen...  16.8 us
    dot_general x1, matrix products, on_device(): lax.dot_general(all_rows, weights, (((1,), (1,)), ((), ())), preferred_el...  16.4 us
    broadcast_in_dim x1, other arithmetic, on_device(): return (grad_rows[None], grad_weight.astype(jnp.bfloat16)[None], grad_probs)  6.83 us
    all_to_all x1, waiting for transfers between devices, on_device(): lax.all_to_all(own_probs.reshape(expert_count, capacity), 'expert', split...  5.49 us
  transfers between devices with their start and end apart: 3, of which 3 were waited for; matrix products, arithmetic and copies ran while one was open for 3% of the time, Pallas kernels for 0%

commit v1 on v0

v1 whole, which is shorter than its diff:
```python
import functools

import jax
import jax.numpy as jnp
from jax import lax
from jax.experimental import pallas as pl
from jax.experimental.pallas import tpu as pltpu
from jax.sharding import PartitionSpec as P

MESH = pl.DeviceIdType.MESH
LANES = 128
SUB = 8
F32 = jnp.float32
BF16 = jnp.bfloat16


def iota(shape, axis):
    return lax.broadcasted_iota(jnp.int32, shape, axis)


def as_row(column, lanes):
    shape = (column.shape[0], lanes)
    return jnp.sum(jnp.where(iota(shape, 0) == iota(shape, 1), column, 0), axis=0, keepdims=True)


def as_column(row, count):
    shape = (count, row.shape[1])
    return jnp.sum(jnp.where(iota(shape, 0) == iota(shape, 1), row, 0), axis=1, keepdims=True)


def flip(index, bits):
    bit = 1
    while bit <= bits:
        if bits & bit:
            index = index + bit * (1 - 2 * ((index // bit) % 2))
        bit *= 2
    return index


def pack_kernel(n_e, cap, x_ref, probs_ref, routes_ref, rows_ref, p_ref, dest_ref):
    tokens, top = routes_ref.shape
    routes = routes_ref[...]
    probs = probs_ref[...].astype(F32)
    route_rows = [as_row(routes[:, k : k + 1], tokens) for k in range(top)]
    prob_rows = [as_row(probs[:, k : k + 1], tokens) for k in range(top)]
    square = (tokens, tokens)
    before = iota(square, 0) < iota(square, 1)
    expert = iota((2 * SUB, tokens), 0)
    named = sum((expert == r).astype(F32) for r in route_rows)
    rank = jnp.dot(named.astype(BF16), before.astype(BF16), preferred_element_type=F32)
    rank = rank.astype(jnp.int32)
    x = x_ref[...]
    places = iota((cap, tokens), 0)
    dest = [jnp.zeros((1, tokens), jnp.int32) for _ in range(top)]
    for e in range(n_e):
        names = sum((r == e).astype(jnp.int32) for r in route_rows)
        weight = sum(jnp.where(r == e, p, 0.0) for r, p in zip(route_rows, prob_rows))
        rank_e = rank[e : e + 1, :]
        chosen = (places == rank_e) & (names > 0)
        rows_ref[e] = jnp.dot(chosen.astype(F32).astype(BF16), x, preferred_element_type=F32).astype(BF16)
        p_column = jnp.sum(jnp.where(chosen, weight, 0.0), axis=1, keepdims=True)
        p_ref[e] = jnp.broadcast_to(as_row(p_column, LANES), (SUB, LANES))
        for k in range(top):
            dest[k] = dest[k] + jnp.where(route_rows[k] == e, rank_e + e * LANES, 0)
    lane = iota((tokens, top), 1)
    out = jnp.zeros((tokens, top), jnp.int32)
    for k in range(top):
        out = jnp.where(lane == k, as_column(dest[k], tokens), out)
    dest_ref[...] = out


def main_kernel(
    n_e, n_d, cap,
    sent_ref, sentp_ref, dest_ref, hidden_ref, w_ref,
    gh_ref, gd_ref, gp_ref,
    rows, wv, wt, hbuf, gbuf, ht, scaled, acc, gdb,
    pz, pall, sbuf, sall, tot, tall,
    z_send, z_recv, b_send, b_recv, p_send, p_recv, q_send, q_recv,
    s_send, s_recv, t_send, t_recv, local, h_sem, g_sem, d_sem,
):
    d, z = lax.axis_index("dp"), lax.axis_index("expert")
    depth = w_ref.shape[1]
    half = depth // 2
    width = depth // d_sem.shape[0]
    ch = n_d // 2
    dc, dx, dy = flip(d, 1), flip(d, 2), flip(d, 4)
    dd = flip(d, 6)

    barrier = pltpu.get_barrier_semaphore()
    for k in range(1, n_e):
        pl.semaphore_signal(barrier, inc=1, device_id=(d, flip(z, k)), device_id_type=MESH)
    for j in range(1, n_d):
        pl.semaphore_signal(barrier, inc=1, device_id=(flip(d, j), z), device_id_type=MESH)
    w_copy = pltpu.make_async_copy(w_ref, wv, local.at[0])
    own_copy = pltpu.make_async_copy(sent_ref.at[z], rows.at[0, d], local.at[1])
    ownp_copy = pltpu.make_async_copy(sentp_ref.at[z], pz.at[0], local.at[2])
    own_copy.start()
    ownp_copy.start()
    w_copy.start()

    def h_copy(k):
        return pltpu.make_async_copy(hidden_ref.at[:, flip(z, k)], hbuf.at[k % 2], h_sem.at[k % 2])

    def g_copy(k):
        return pltpu.make_async_copy(gbuf.at[k % 2], gh_ref.at[:, flip(z, k)], g_sem.at[k % 2])

    h_copy(0).start()
    h_copy(1).start()
    pl.semaphore_wait(barrier, n_e + n_d - 2)

    def remote(src, dst, send, recv, to):
        return pltpu.make_async_remote_copy(
            src_ref=src, dst_ref=dst, send_sem=send, recv_sem=recv, device_id=to, device_id_type=MESH
        )

    def z_copy(k):
        to = flip(z, k)
        return remote(sent_ref.at[to], rows.at[k, d], z_send.at[k], z_recv.at[k], (d, to))

    def p_copy(k):
        to = flip(z, k)
        return remote(sentp_ref.at[to], pz.at[k], p_send.at[k], p_recv.at[k], (d, to))

    def q_copy(j):
        return remote(pz, pall.at[d], q_send.at[j], q_recv.at[j], (flip(d, j), z))

    def s_copy(j):
        to = flip(d, j)
        return remote(sbuf.at[to], sall.at[j], s_send.at[j], s_recv.at[j], (to, z))

    def t_copy(k):
        return remote(tot, tall.at[k], t_send.at[k], t_recv.at[k], (d, flip(z, k)))

    lo, hi = pl.ds(0, half), pl.ds(half, half)

    def b_copy(k, kind):
        whole = slice(None)
        src, cols, to = {
            0: (d, whole, dx),
            1: (d, whole, dy),
            2: (d, whole, dc),
            3: (dx, lo, dy),
            4: (dy, hi, dx),
            5: (dx, whole, dc),
            6: (dy, whole, dc),
            7: (dd, lo, dc),
            8: (dd, hi, dc),
        }[kind]
        part = rows.at[k, src] if cols is whole else rows.at[k, src, :, cols]
        return remote(part, part, b_send.at[k, kind], b_recv.at[k, kind], (to, z))

    def own_step(k):
        if k == 0:
            own_copy.wait()
        else:
            z_copy(k).wait_recv()
        for kind in (0, 1, 2):
            b_copy(k, kind).start()

    def side_step(k):
        b_copy(k, 0).wait_recv()
        b_copy(k, 3).start()
        b_copy(k, 5).start()
        b_copy(k, 1).wait_recv()
        b_copy(k, 4).start()
        b_copy(k, 6).start()

    def diagonal_step(k):
        b_copy(k, 3).wait_recv()
        b_copy(k, 7).start()
        b_copy(k, 4).wait_recv()
        b_copy(k, 8).start()

    def partner_step(k):
        for kind in (2, 5, 6, 7, 8):
            b_copy(k, kind).wait_recv()

    for k in range(1, n_e):
        p_copy(k).start()
    own_step(0)
    for k in range(1, n_e):
        z_copy(k).start()

    w_copy.wait()
    tile = 256 if depth % 256 == 0 else LANES

    @pl.loop(0, depth // tile)
    def _(i):
        at = pl.ds(pl.multiple_of(i * tile, tile), tile)
        wt[at, :] = wv[:, at].T

    ownp_copy.wait()
    for k in range(1, n_e):
        p_copy(k).wait_recv()
    for j in range(1, n_d):
        q_copy(j).start()
    own_p = pltpu.make_async_copy(pz, pall.at[d], local.at[3])
    own_p.start()
    own_step(1)
    side_step(0)
    own_p.wait()
    for j in range(1, n_d):
        q_copy(j).wait_recv()
    sbuf[...] = jnp.zeros_like(sbuf)

    for k in range(n_e):
        diagonal_step(k)
        partner_step(k)
        h_copy(k).wait()
        if k >= 2:
            g_copy(k - 2).wait()
        ht[...] = hbuf[k % 2].reshape(n_d * cap, -1).T

        @pl.loop(0, 2)
        def _(i):
            group = pl.ds(i * ch, ch)
            r = rows[k, group].reshape(ch * cap, depth)
            back = jnp.dot(r, wt[...], preferred_element_type=F32)
            p = jnp.concatenate([as_column(pall[i * ch + j, k, 0:1, :], cap) for j in range(ch)], axis=0)
            scaled[group] = (p * r.astype(F32)).astype(BF16).reshape(ch, cap, depth)
            gbuf[k % 2, group] = (p * back).astype(BF16).reshape(ch, cap, -1)
            h = hbuf[k % 2, group].reshape(ch * cap, -1).astype(F32)
            slot = jnp.sum(h * back, axis=1, keepdims=True)
            for j in range(ch):
                sbuf[i * ch + j, k : k + 1, :] = as_row(slot[j * cap : (j + 1) * cap], LANES)

        g_copy(k).start()
        if k + 2 < n_e:
            own_step(k + 2)
        if k + 1 < n_e:
            side_step(k + 1)
        else:
            for j in range(1, n_d):
                s_copy(j).start()

        @pl.loop(0, depth // width)
        def _(i):
            at = pl.ds(pl.multiple_of(i * width, width), width)
            part = jnp.dot(
                ht[...], scaled[:, :, at].reshape(n_d * cap, width), preferred_element_type=F32
            )
            if k > 0:
                part = acc[:, at] + part
            if k < n_e - 1:
                acc[:, at] = part
            else:
                gdb[:, at] = part.astype(BF16)
                pltpu.make_async_copy(gdb.at[:, at], gd_ref.at[:, at], d_sem.at[i]).start()

        if k + 2 < n_e:
            h_copy(k + 2).start()

    total = sbuf[d]
    for j in range(1, n_d):
        s_copy(j).wait_recv()
        total = total + sall[j]
    tot[...] = total
    for k in range(1, n_e):
        t_copy(k).start()
    tokens, top = dest_ref.shape
    lane = iota((tokens, top), 1)
    lanes = iota((tokens, LANES), 1)
    result = jnp.zeros((tokens, top), F32)
    for k in range(n_e):
        if k > 0:
            t_copy(k).wait_recv()
            row = tall[k][k : k + 1, :]
        else:
            row = total[0:1, :]
        base = flip(z, k) * LANES
        for t in range(top):
            hit = dest_ref[:, t : t + 1] == base + lanes
            value = jnp.sum(jnp.where(hit, row, 0.0), axis=1, keepdims=True)
            result = result + jnp.where(lane == t, value, 0.0)
    gp_ref[...] = result

    for k in range(1, n_e):
        z_copy(k).wait_send()
        p_copy(k).wait_send()
        t_copy(k).wait_send()
    for j in range(1, n_d):
        q_copy(j).wait_send()
        s_copy(j).wait_send()
    for k in range(n_e):
        for kind in range(9):
            b_copy(k, kind).wait_send()
    for k in range(max(0, n_e - 2), n_e):
        g_copy(k).wait()

    @pl.loop(0, depth // width)
    def _(i):
        at = pl.ds(pl.multiple_of(i * width, width), width)
        pltpu.make_async_copy(gdb.at[:, at], gd_ref.at[:, at], d_sem.at[i]).wait()


def on_device(grad_out, probs, routes, hidden, w_down):
    n_e, n_d = lax.axis_size("expert"), lax.axis_size("dp")
    tokens, top = routes.shape
    cap = tokens * top * 5 // (4 * n_e)
    depth = grad_out.shape[1]
    units = hidden.shape[2]
    slots = n_d * cap
    vmem = pl.BlockSpec(memory_space=pltpu.VMEM)
    hbm = pl.BlockSpec(memory_space=pl.ANY)
    rows, p, dest = pl.pallas_call(
        functools.partial(pack_kernel, n_e, cap),
        out_shape=(
            jax.ShapeDtypeStruct((n_e, cap, depth), BF16),
            jax.ShapeDtypeStruct((n_e, SUB, LANES), F32),
            jax.ShapeDtypeStruct((tokens, top), jnp.int32),
        ),
        in_specs=[vmem] * 3,
        out_specs=(vmem, vmem, vmem),
        name="pack",
    )(grad_out, probs, routes)
    dma = pltpu.SemaphoreType.DMA
    chunks = max(1, depth // 256)
    gh, gd, gp = pl.pallas_call(
        functools.partial(main_kernel, n_e, n_d, cap),
        out_shape=(
            jax.ShapeDtypeStruct((n_d, n_e, cap, units), BF16),
            jax.ShapeDtypeStruct((units, depth), BF16),
            jax.ShapeDtypeStruct((tokens, top), F32),
        ),
        in_specs=[hbm, hbm, vmem, hbm, hbm],
        out_specs=(hbm, hbm, vmem),
        scratch_shapes=[
            pltpu.VMEM((n_e, n_d, cap, depth), BF16),
            pltpu.VMEM((units, depth), BF16),
            pltpu.VMEM((depth, units), BF16),
            pltpu.VMEM((2, n_d, cap, units), BF16),
            pltpu.VMEM((2, n_d, cap, units), BF16),
            pltpu.VMEM((units, slots), BF16),
            pltpu.VMEM((n_d, cap, depth), BF16),
            pltpu.VMEM((units, depth), F32),
            pltpu.VMEM((units, depth), BF16),
            pltpu.VMEM((n_e, SUB, LANES), F32),
            pltpu.VMEM((n_d, n_e, SUB, LANES), F32),
            pltpu.VMEM((n_d, SUB, LANES), F32),
            pltpu.VMEM((n_d, SUB, LANES), F32),
            pltpu.VMEM((SUB, LANES), F32),
            pltpu.VMEM((n_e, SUB, LANES), F32),
            dma((n_e,)), dma((n_e,)),
            dma((n_e, 9)), dma((n_e, 9)),
            dma((n_e,)), dma((n_e,)),
            dma((n_d,)), dma((n_d,)),
            dma((n_d,)), dma((n_d,)),
            dma((n_e,)), dma((n_e,)),
            dma((4,)), dma((2,)), dma((2,)), dma((chunks,)),
        ],
        compiler_params=pltpu.CompilerParams(
            collective_id=0, has_side_effects=True, vmem_limit_bytes=62 * 1024 * 1024
        ),
        name="expert_back",
    )(rows, p, dest, hidden[0].reshape(n_d, n_e, cap, units), w_down[0])
    return gh.reshape(1, n_d * n_e * cap, units), gd[None], gp


def solution(mesh):
    in_specs = (
        P(("dp", "expert"), None),
        P(("dp", "expert"), None),
        P(("dp", "expert"), None),
        P("expert", None, "dp"),
        P("expert", "dp", None),
    )
    out_specs = (P("expert", None, "dp"), P("expert", "dp", None), P(("dp", "expert"), None))
    return jax.shard_map(
        on_device, mesh=mesh, in_specs=in_specs, out_specs=out_specs, check_vma=False
    )
```

time: 231 us -> 111 us (0.48)
  Pallas kernels: 0 us -> 99 us
  blocking collectives: 73.3 us -> 0 us
  waiting for transfers between devices: 64.2 us -> 0 us
  matrix products: 33.7 us -> 0 us
  between operations: 15.4 us -> 0.64 us
  local copies, waits for them, and re-layouts: 25.1 us -> 11.1 us
  other arithmetic: 10.3 us -> 0 us
  starting transfers between devices: 7.86 us -> 0 us
    pallas_call x0 -> x2, Pallas kernels: none -> 99 us  [the longest x1 96.2 us: on_device(): pl.pallas_call(functools.partial(main_kernel, n_e, n_d, cap), out_shape=(...]
    all_gather x1 -> x0, waiting for transfers between devices: 53.8 us -> none  [on_device(): lax.all_gather(block_rows, 'dp', axis=0, tiled=True)]
    all_to_all x1 -> x0, blocking collectives: 37.6 us -> none  [on_device(): lax.all_to_all(sent_rows.reshape(expert_count, capacity, width), 'expert'...]
    unnamed x2 -> x0, blocking collectives: 35.7 us -> none
    dot_general x3 -> x0, matrix products: 33.7 us -> none  [the longest x1 16.8 us: on_device(): lax.dot_general(saved, scaled, (((0,), (0,)), ((), ())), preferred_elemen...]
    unnamed x14 -> x7, local copies, waits for them, and re-layouts: 22.3 us -> 11.1 us
    all_to_all x2 -> x0, waiting for transfers between devices: 10.4 us -> none  [the longest x1 5.49 us: on_device(): lax.all_to_all(own_probs.reshape(expert_count, capacity), 'expert', split...]
    all_to_all x2 -> x0, starting transfers between devices: 7.82 us -> none  [the longest x1 4.6 us: on_device(): lax.all_to_all(own_probs.reshape(expert_count, capacity), 'expert', split...]
  transfers between devices with their start and end apart: 3 -> 0, of which waited for: 3 -> 0; matrix products, arithmetic and copies ran while one was open for 3% -> 0% of each run, Pallas kernels for 0% -> 0%
where the time goes in v1:
time: 111 us
  Pallas kernels  99 us (89%)
  local copies, waits for them, and re-layouts  11.1 us (10%)
    pallas_call x1, Pallas kernels, on_device(): pl.pallas_call(functools.partial(main_kernel, n_e, n_d, cap), out_shape=(...  96.2 us
    unnamed x7, local copies, waits for them, and re-layouts  11.1 us
    pallas_call x1, Pallas kernels, on_device(): pl.pallas_call(functools.partial(pack_kernel, n_e, cap), out_shape=(jax.S...  2.85 us

profile of v1, /device:TPU:0, one launch (start us, length us, event | category | flops | bytes accessed | tf_op | source)
XLA Modules:
  0.0 110.8 jit_solution(5314824486962075115)
XLA Ops:
  0.6 1.4 %copy.8.probs_ref = bf16[128,2]{1,0:T(8,128)(2,1)} copy(bf16[128,2]{0,1:T(2,128)(2,1)} %param.6) | data formatting | bytes 1024 | tf_op args[1]
  2.0 1.4 %copy.9.routes_ref = s32[128,2]{1,0:T(8,128)} copy(s32[128,2]{0,1:T(2,128)} %param.7) | data formatting | bytes 2048 | tf_op args[2]
  3.4 2.9 %pack.1 = (bf16[4,80,2048]{2,1,0:T(8,128)(2,1)}, f32[4,8,128]{2,1,0:T(8,128)}, s32[128,2]{1,0:T(8,128)}) custom-call(bf16[128,2048]{1,0:T(8,128)(2,1)} %x_ref.1, bf16[128,2]{1,0:T(8,128)(2,1)} %copy.8.probs_ref, s32[128,2]{1,0:T(8,128)} %copy.9.routes_ref), custom_call_target="tpu_custom_call" | custom-call | tf_op jit(solution)/shard_map/pack/pallas_call | solution.py:305
  6.3 96.2 %expert_back.1 = (bf16[8,4,80,896]{3,2,1,0:T(8,128)(2,1)}, bf16[896,2048]{1,0:T(8,128)(2,1)}, f32[128,2]{1,0:T(8,128)}) custom-call(bf16[4,80,2048]{2,1,0:T(8,128)(2,1)} %get-tuple-element.9.sent_ref, f32[4,8,128]{2,1,0:T(8,128)} %get-tuple-element.10.sentp_ref, s32[128,2]{1,0:T(8,128)} %get-tuple-element.11.dest_ref, bf16[8,4,80,896]{3,2,1,0:T(8,128)(2,1)} %bitcast.4, ...), custom_call_target="tpu_custom_call" | custom-call | tf_op jit(solution)/shard_map/expert_back/pallas_call | solution.py:318
  102.5 1.5 %copy.10 = f32[128,2]{0,1:T(2,128)} copy(f32[128,2]{1,0:T(8,128)} %get-tuple-element.17) | data formatting | bytes 2048
  104.0 0.0 copy-start
  104.0 5.0 %copy.13 = bf16[1,2560,896]{2,1,0:T(8,128)(2,1)} copy(bf16[1,2560,896]{2,1,0:T(8,128)(2,1)} %bitcast.5) | data formatting | bytes 9175040
  108.9 0.0 copy-done
  108.9 1.8 %copy.14 = bf16[1,896,2048]{2,1,0:T(8,128)(2,1)} copy(bf16[1,896,2048]{2,1,0:T(8,128)(2,1)S(1)} %bitcast.6) | data formatting | bytes 7340032
Async XLA Ops:
  104.0 5.0 %copy-start = (bf16[896,2048]{1,0:T(8,128)(2,1)S(1)}, bf16[896,2048]{1,0:T(8,128)(2,1)}, u32[]{:S(2)}) copy-start(bf16[896,2048]{1,0:T(8,128)(2,1)} %get-tuple-element.13) | copy-start | bytes 11010052

commit v2 on v1

--- a/solution.py
+++ b/solution.py
@@ -38,11 +38,10 @@
 
 
 def pack_kernel(n_e, cap, x_ref, probs_ref, routes_ref, rows_ref, p_ref, dest_ref):
-    tokens, top = routes_ref.shape
-    routes = routes_ref[...]
+    top, tokens = routes_ref.shape
     probs = probs_ref[...].astype(F32)
-    route_rows = [as_row(routes[:, k : k + 1], tokens) for k in range(top)]
-    prob_rows = [as_row(probs[:, k : k + 1], tokens) for k in range(top)]
+    route_rows = [routes_ref[k : k + 1, :] for k in range(top)]
+    prob_rows = [probs[k : k + 1, :] for k in range(top)]
     square = (tokens, tokens)
     before = iota(square, 0) < iota(square, 1)
     expert = iota((2 * SUB, tokens), 0)
@@ -62,18 +61,15 @@
         p_ref[e] = jnp.broadcast_to(as_row(p_column, LANES), (SUB, LANES))
         for k in range(top):
             dest[k] = dest[k] + jnp.where(route_rows[k] == e, rank_e + e * LANES, 0)
-    lane = iota((tokens, top), 1)
-    out = jnp.zeros((tokens, top), jnp.int32)
     for k in range(top):
-        out = jnp.where(lane == k, as_column(dest[k], tokens), out)
-    dest_ref[...] = out
+        dest_ref[k : k + 1, :] = dest[k]
 
 
 def main_kernel(
     n_e, n_d, cap,
     sent_ref, sentp_ref, dest_ref, hidden_ref, w_ref,
     gh_ref, gd_ref, gp_ref,
-    rows, wv, wt, hbuf, gbuf, ht, scaled, acc, gdb,
+    rows, wv, wt, hbuf, gbuf, ht, ht_last, scaled, acc, gdb,
     pz, pall, sbuf, sall, tot, tall,
     z_send, z_recv, b_send, b_recv, p_send, p_recv, q_send, q_recv,
     s_send, s_recv, t_send, t_recv, local, h_sem, g_sem, d_sem,
@@ -82,7 +78,6 @@
     depth = w_ref.shape[1]
     half = depth // 2
     width = depth // d_sem.shape[0]
-    ch = n_d // 2
     dc, dx, dy = flip(d, 1), flip(d, 2), flip(d, 4)
     dd = flip(d, 6)
 
@@ -98,11 +93,38 @@
     ownp_copy.start()
     w_copy.start()
 
+    groups = n_d // 2
+
+    def pair(g):
+        return 2 * flip(d // 2, g)
+
+    class Parts:
+        def __init__(self, parts):
+            self.parts = parts
+
+        def start(self):
+            for part in self.parts:
+                part.start()
+
+        def wait(self):
+            for part in self.parts:
+                part.wait()
+
     def h_copy(k):
-        return pltpu.make_async_copy(hidden_ref.at[:, flip(z, k)], hbuf.at[k % 2], h_sem.at[k % 2])
-
-    def g_copy(k):
-        return pltpu.make_async_copy(gbuf.at[k % 2], gh_ref.at[:, flip(z, k)], g_sem.at[k % 2])
+        return Parts([
+            pltpu.make_async_copy(
+                hidden_ref.at[pl.ds(pair(g), 2), flip(z, k)], hbuf.at[k % 2, pl.ds(2 * g, 2)], h_sem.at[k % 2, g]
+            )
+            for g in range(groups)
+        ])
+
+    def g_copy(k, gs=range(n_d // 2)):
+        return Parts([
+            pltpu.make_async_copy(
+                gbuf.at[k % 2, pl.ds(2 * g, 2)], gh_ref.at[pl.ds(pair(g), 2), flip(z, k)], g_sem.at[k % 2, g]
+            )
+            for g in gs
+        ])
 
     h_copy(0).start()
     h_copy(1).start()
@@ -171,15 +193,14 @@
         b_copy(k, 4).wait_recv()
         b_copy(k, 8).start()
 
-    def partner_step(k):
-        for kind in (2, 5, 6, 7, 8):
+    def partner_step(k, kinds):
+        for kind in kinds:
             b_copy(k, kind).wait_recv()
 
     for k in range(1, n_e):
+        z_copy(k).start()
         p_copy(k).start()
     own_step(0)
-    for k in range(1, n_e):
-        z_copy(k).start()
 
     w_copy.wait()
     tile = 256 if depth % 256 == 0 else LANES
@@ -196,59 +217,82 @@
         q_copy(j).start()
     own_p = pltpu.make_async_copy(pz, pall.at[d], local.at[3])
     own_p.start()
-    own_step(1)
-    side_step(0)
+    sbuf[...] = jnp.zeros_like(sbuf)
     own_p.wait()
     for j in range(1, n_d):
         q_copy(j).wait_recv()
-    sbuf[...] = jnp.zeros_like(sbuf)
+
+    def back_step(k, gs):
+        first, count = 2 * gs[0], 2 * len(gs)
+        members = [pair(g) + c for g in gs for c in range(2)]
+        r = jnp.concatenate([rows[k, m] for m in members], axis=0)
+        back = jnp.dot(r, wt[...], preferred_element_type=F32)
+        p = jnp.concatenate([as_column(pall[m, k, 0:1, :], cap) for m in members], axis=0)
+        at = pl.ds(first, count)
+        scaled[at] = (p * r.astype(F32)).astype(BF16).reshape(count, cap, depth)
+        gbuf[k % 2, at] = (p * back).astype(BF16).reshape(count, cap, -1)
+        h = hbuf[k % 2, at].reshape(count * cap, -1).astype(F32)
+        slot = jnp.sum(h * back, axis=1, keepdims=True)
+        for j, m in enumerate(members):
+            sbuf[m, k : k + 1, :] = as_row(slot[j * cap : (j + 1) * cap], LANES)
+        g_copy(k, gs).start()
+
+    def weight_step(k, first, count, turned, add, final, start=0, stop=depth // width):
+        @pl.loop(start, stop)
+        def _(i):
+            at = pl.ds(pl.multiple_of(i * width, width), width)
+            part = jnp.dot(
+                turned[:, 0 : count * cap],
+                scaled[first : first + count, :, at].reshape(count * cap, width),
+                preferred_element_type=F32,
+            )
+            if add:
+                part = acc[:, at] + part
+            if final:
+                gdb[:, at] = part.astype(BF16)
+                pltpu.make_async_copy(gdb.at[:, at], gd_ref.at[:, at], d_sem.at[i]).start()
+            else:
+                acc[:, at] = part
 
     for k in range(n_e):
-        diagonal_step(k)
-        partner_step(k)
+        last = k == n_e - 1
         h_copy(k).wait()
         if k >= 2:
             g_copy(k - 2).wait()
-        ht[...] = hbuf[k % 2].reshape(n_d * cap, -1).T
-
-        @pl.loop(0, 2)
-        def _(i):
-            group = pl.ds(i * ch, ch)
-            r = rows[k, group].reshape(ch * cap, depth)
-            back = jnp.dot(r, wt[...], preferred_element_type=F32)
-            p = jnp.concatenate([as_column(pall[i * ch + j, k, 0:1, :], cap) for j in range(ch)], axis=0)
-            scaled[group] = (p * r.astype(F32)).astype(BF16).reshape(ch, cap, depth)
-            gbuf[k % 2, group] = (p * back).astype(BF16).reshape(ch, cap, -1)
-            h = hbuf[k % 2, group].reshape(ch * cap, -1).astype(F32)
-            slot = jnp.sum(h * back, axis=1, keepdims=True)
-            for j in range(ch):
-                sbuf[i * ch + j, k : k + 1, :] = as_row(slot[j * cap : (j + 1) * cap], LANES)
-
-        g_copy(k).start()
+        if k == 0:
+            partner_step(0, (2,))
+            back_step(0, (0,))
+            own_step(1)
+            side_step(0)
+            partner_step(0, (5,))
+            back_step(0, (1,))
+        else:
+            partner_step(k, (2, 5))
+            back_step(k, (0, 1))
+        diagonal_step(k)
         if k + 2 < n_e:
             own_step(k + 2)
-        if k + 1 < n_e:
+        partner_step(k, (6,))
+        if not last:
+            ht[...] = hbuf[k % 2].reshape(n_d * cap, -1).T
+            partner_step(k, (7, 8))
+            back_step(k, (2, 3))
             side_step(k + 1)
+            weight_step(k, 0, n_d, ht, k > 0, False)
+            if k + 2 < n_e:
+                h_copy(k + 2).start()
         else:
+            back_step(k, (2,))
+            most = n_d - 2
+            ht[:, 0 : most * cap] = hbuf[k % 2, 0:most].reshape(most * cap, -1).T
+            ht_last[...] = hbuf[k % 2, most:n_d].reshape(2 * cap, -1).T
+            weight_step(k, 0, most, ht, k > 0, False)
+            partner_step(k, (7, 8))
+            back_step(k, (3,))
+            weight_step(k, most, 2, ht_last, True, True, 0, 1)
             for j in range(1, n_d):
                 s_copy(j).start()
-
-        @pl.loop(0, depth // width)
-        def _(i):
-            at = pl.ds(pl.multiple_of(i * width, width), width)
-            part = jnp.dot(
-                ht[...], scaled[:, :, at].reshape(n_d * cap, width), preferred_element_type=F32
-            )
-            if k > 0:
-                part = acc[:, at] + part
-            if k < n_e - 1:
-                acc[:, at] = part
-            else:
-                gdb[:, at] = part.astype(BF16)
-                pltpu.make_async_copy(gdb.at[:, at], gd_ref.at[:, at], d_sem.at[i]).start()
-
-        if k + 2 < n_e:
-            h_copy(k + 2).start()
+            weight_step(k, most, 2, ht_last, True, True, 1)
 
     total = sbuf[d]
     for j in range(1, n_d):
@@ -257,22 +301,22 @@
     tot[...] = total
     for k in range(1, n_e):
         t_copy(k).start()
-    tokens, top = dest_ref.shape
-    lane = iota((tokens, top), 1)
-    lanes = iota((tokens, LANES), 1)
-    result = jnp.zeros((tokens, top), F32)
+    top, tokens = dest_ref.shape
+    lanes = iota((LANES, tokens), 0)
+    result = [jnp.zeros((1, tokens), F32) for _ in range(top)]
     for k in range(n_e):
         if k > 0:
             t_copy(k).wait_recv()
             row = tall[k][k : k + 1, :]
         else:
             row = total[0:1, :]
+        column = as_column(row, LANES)
         base = flip(z, k) * LANES
         for t in range(top):
-            hit = dest_ref[:, t : t + 1] == base + lanes
-            value = jnp.sum(jnp.where(hit, row, 0.0), axis=1, keepdims=True)
-            result = result + jnp.where(lane == t, value, 0.0)
-    gp_ref[...] = result
+            hit = dest_ref[t : t + 1, :] == base + lanes
+            result[t] = result[t] + jnp.sum(jnp.where(hit, column, 0.0), axis=0, keepdims=True)
+    for t in range(top):
+        gp_ref[t : t + 1, :] = result[t]
 
     for k in range(1, n_e):
         z_copy(k).wait_send()
@@ -307,12 +351,12 @@
         out_shape=(
             jax.ShapeDtypeStruct((n_e, cap, depth), BF16),
             jax.ShapeDtypeStruct((n_e, SUB, LANES), F32),
-            jax.ShapeDtypeStruct((tokens, top), jnp.int32),
+            jax.ShapeDtypeStruct((top, tokens), jnp.int32),
         ),
         in_specs=[vmem] * 3,
         out_specs=(vmem, vmem, vmem),
         name="pack",
-    )(grad_out, probs, routes)
+    )(grad_out, probs.T, routes.T)
     dma = pltpu.SemaphoreType.DMA
     chunks = max(1, depth // 256)
     gh, gd, gp = pl.pallas_call(
@@ -320,7 +364,7 @@
         out_shape=(
             jax.ShapeDtypeStruct((n_d, n_e, cap, units), BF16),
             jax.ShapeDtypeStruct((units, depth), BF16),
-            jax.ShapeDtypeStruct((tokens, top), F32),
+            jax.ShapeDtypeStruct((top, tokens), F32),
         ),
         in_specs=[hbm, hbm, vmem, hbm, hbm],
         out_specs=(hbm, hbm, vmem),
@@ -331,6 +375,7 @@
             pltpu.VMEM((2, n_d, cap, units), BF16),
             pltpu.VMEM((2, n_d, cap, units), BF16),
             pltpu.VMEM((units, slots), BF16),
+            pltpu.VMEM((units, 2 * cap), BF16),
             pltpu.VMEM((n_d, cap, depth), BF16),
             pltpu.VMEM((units, depth), F32),
             pltpu.VMEM((units, depth), BF16),
@@ -346,14 +391,14 @@
             dma((n_d,)), dma((n_d,)),
             dma((n_d,)), dma((n_d,)),
             dma((n_e,)), dma((n_e,)),
-            dma((4,)), dma((2,)), dma((2,)), dma((chunks,)),
+            dma((4,)), dma((2, n_d // 2)), dma((2, n_d // 2)), dma((chunks,)),
         ],
         compiler_params=pltpu.CompilerParams(
             collective_id=0, has_side_effects=True, vmem_limit_bytes=62 * 1024 * 1024
         ),
         name="expert_back",
     )(rows, p, dest, hidden[0].reshape(n_d, n_e, cap, units), w_down[0])
-    return gh.reshape(1, n_d * n_e * cap, units), gd[None], gp
+    return gh.reshape(1, n_d * n_e * cap, units), gd[None], gp.T
 
 
 def solution(mesh):

time: 111 us -> 110 us (level)
  local copies, waits for them, and re-layouts: 11.1 us -> 7.36 us
  Pallas kernels: 99 us -> 102 us
    unnamed x7, local copies, waits for them, and re-layouts: 11.1 us -> 7.36 us
    pallas_call x1, Pallas kernels: 96.2 us -> 99.2 us  [on_device(): pl.pallas_call(functools.partial(main_kernel, n_e, n_d, cap), out_shape=(...]
where the time goes in v2:
time: 110 us
  Pallas kernels  102 us (93%)
  local copies, waits for them, and re-layouts  7.36 us (7%)
    pallas_call x1, Pallas kernels, on_device(): pl.pallas_call(functools.partial(main_kernel, n_e, n_d, cap), out_shape=(...  99.2 us
    unnamed x7, local copies, waits for them, and re-layouts  7.36 us
    pallas_call x1, Pallas kernels, on_device(): pl.pallas_call(functools.partial(pack_kernel, n_e, cap), out_shape=(jax.S...  2.76 us

profile of v2, /device:TPU:0, one launch (start us, length us, event | category | flops | bytes accessed | tf_op | source)
XLA Modules:
  0.0 109.9 jit_solution(18094352265316927137)
XLA Ops:
  0.6 2.8 %pack.1 = (bf16[4,80,2048]{2,1,0:T(8,128)(2,1)}, f32[4,8,128]{2,1,0:T(8,128)}, s32[2,128]{1,0:T(2,128)}) custom-call(bf16[128,2048]{1,0:T(8,128)(2,1)} %x_ref.1, bf16[2,128]{1,0:T(2,128)(2,1)} %bitcast.13, s32[2,128]{1,0:T(2,128)} %bitcast.11), custom_call_target="tpu_custom_call" | custom-call | tf_op jit(solution)/shard_map/pack/pallas_call | solution.py:349
  3.4 99.2 %expert_back.1 = (bf16[8,4,80,896]{3,2,1,0:T(8,128)(2,1)}, bf16[896,2048]{1,0:T(8,128)(2,1)}, f32[2,128]{1,0:T(2,128)}) custom-call(bf16[4,80,2048]{2,1,0:T(8,128)(2,1)} %get-tuple-element.9.sent_ref, f32[4,8,128]{2,1,0:T(8,128)} %get-tuple-element.10.sentp_ref, s32[2,128]{1,0:T(2,128)} %get-tuple-element.11.dest_ref, bf16[8,4,80,896]{3,2,1,0:T(8,128)(2,1)} %bitcast.7, ...), custom_call_target="tpu_custom_call" | custom-call | tf_op jit(solution)/shard_map/expert_back/pallas_call | solution.py:362
  102.6 0.0 copy-start
  102.6 5.0 %copy.11 = bf16[1,2560,896]{2,1,0:T(8,128)(2,1)} copy(bf16[1,2560,896]{2,1,0:T(8,128)(2,1)} %bitcast.8) | data formatting | bytes 9175040
  107.5 0.0 copy-done
  107.5 0.0 copy-start.1
  107.5 1.8 %copy.12 = bf16[1,896,2048]{2,1,0:T(8,128)(2,1)} copy(bf16[1,896,2048]{2,1,0:T(8,128)(2,1)S(1)} %bitcast.9) | data formatting | bytes 7340032
  109.4 0.0 copy-done.1
  109.4 0.6 copy.13
Async XLA Ops:
  102.6 5.0 %copy-start = (bf16[896,2048]{1,0:T(8,128)(2,1)S(1)}, bf16[896,2048]{1,0:T(8,128)(2,1)}, u32[]{:S(2)}) copy-start(bf16[896,2048]{1,0:T(8,128)(2,1)} %get-tuple-element.13) | copy-start | bytes 11010052
  107.5 1.8 %copy-start.1 = (f32[2,128]{1,0:T(2,128)S(1)}, f32[2,128]{1,0:T(2,128)}, u32[]{:S(2)}) copy-start(f32[2,128]{1,0:T(2,128)} %get-tuple-element.14) | copy-start | bytes 3076

commit v3 on v2

--- a/solution.py
+++ b/solution.py
@@ -202,14 +202,6 @@
         p_copy(k).start()
     own_step(0)
 
-    w_copy.wait()
-    tile = 256 if depth % 256 == 0 else LANES
-
-    @pl.loop(0, depth // tile)
-    def _(i):
-        at = pl.ds(pl.multiple_of(i * tile, tile), tile)
-        wt[at, :] = wv[:, at].T
-
     ownp_copy.wait()
     for k in range(1, n_e):
         p_copy(k).wait_recv()
@@ -218,6 +210,16 @@
     own_p = pltpu.make_async_copy(pz, pall.at[d], local.at[3])
     own_p.start()
     sbuf[...] = jnp.zeros_like(sbuf)
+    w_copy.wait()
+    tile = 256 if depth % 256 == 0 else LANES
+
+    @pl.loop(0, depth // tile)
+    def _(i):
+        at = pl.ds(pl.multiple_of(i * tile, tile), tile)
+        wt[at, :] = wv[:, at].T
+
+    own_step(1)
+    side_step(0)
     own_p.wait()
     for j in range(1, n_d):
         q_copy(j).wait_recv()
@@ -254,31 +256,29 @@
             else:
                 acc[:, at] = part
 
+    columns = depth // width
+    early, late = columns * 3 // 8, columns * 3 // 4
     for k in range(n_e):
         last = k == n_e - 1
         h_copy(k).wait()
         if k >= 2:
             g_copy(k - 2).wait()
+        partner_step(k, (2, 5))
+        back_step(k, (0, 1))
         if k == 0:
-            partner_step(0, (2,))
-            back_step(0, (0,))
-            own_step(1)
-            side_step(0)
-            partner_step(0, (5,))
-            back_step(0, (1,))
-        else:
-            partner_step(k, (2, 5))
-            back_step(k, (0, 1))
-        diagonal_step(k)
-        if k + 2 < n_e:
-            own_step(k + 2)
+            diagonal_step(0)
         partner_step(k, (6,))
         if not last:
             ht[...] = hbuf[k % 2].reshape(n_d * cap, -1).T
             partner_step(k, (7, 8))
             back_step(k, (2, 3))
             side_step(k + 1)
-            weight_step(k, 0, n_d, ht, k > 0, False)
+            weight_step(k, 0, n_d, ht, k > 0, False, 0, early)
+            if k + 2 < n_e:
+                own_step(k + 2)
+            weight_step(k, 0, n_d, ht, k > 0, False, early, late)
+            diagonal_step(k + 1)
+            weight_step(k, 0, n_d, ht, k > 0, False, late)
             if k + 2 < n_e:
                 h_copy(k + 2).start()
         else:

time: 110 us -> 110 us (level)
  no operation moved by 1% of the time
where the time goes in v3:
time: 110 us
  Pallas kernels  102 us (93%)
  local copies, waits for them, and re-layouts  7.36 us (7%)
    pallas_call x1, Pallas kernels, on_device(): pl.pallas_call(functools.partial(main_kernel, n_e, n_d, cap), out_shape=(...  99.2 us
    unnamed x7, local copies, waits for them, and re-layouts  7.36 us
    pallas_call x1, Pallas kernels, on_device(): pl.pallas_call(functools.partial(pack_kernel, n_e, cap), out_shape=(jax.S...  2.76 us

profile of v3, /device:TPU:0, one launch (start us, length us, event | category | flops | bytes accessed | tf_op | source)
XLA Modules:
  0.0 110.0 jit_solution(3077357237110214262)
XLA Ops:
  0.6 2.8 %pack.1 = (bf16[4,80,2048]{2,1,0:T(8,128)(2,1)}, f32[4,8,128]{2,1,0:T(8,128)}, s32[2,128]{1,0:T(2,128)}) custom-call(bf16[128,2048]{1,0:T(8,128)(2,1)} %x_ref.1, bf16[2,128]{1,0:T(2,128)(2,1)} %bitcast.13, s32[2,128]{1,0:T(2,128)} %bitcast.11), custom_call_target="tpu_custom_call" | custom-call | tf_op jit(solution)/shard_map/pack/pallas_call | solution.py:349
  3.4 99.2 %expert_back.1 = (bf16[8,4,80,896]{3,2,1,0:T(8,128)(2,1)}, bf16[896,2048]{1,0:T(8,128)(2,1)}, f32[2,128]{1,0:T(2,128)}) custom-call(bf16[4,80,2048]{2,1,0:T(8,128)(2,1)} %get-tuple-element.9.sent_ref, f32[4,8,128]{2,1,0:T(8,128)} %get-tuple-element.10.sentp_ref, s32[2,128]{1,0:T(2,128)} %get-tuple-element.11.dest_ref, bf16[8,4,80,896]{3,2,1,0:T(8,128)(2,1)} %bitcast.7, ...), custom_call_target="tpu_custom_call" | custom-call | tf_op jit(solution)/shard_map/expert_back/pallas_call | solution.py:362
  102.6 0.0 copy-start
  102.6 5.0 %copy.11 = bf16[1,2560,896]{2,1,0:T(8,128)(2,1)} copy(bf16[1,2560,896]{2,1,0:T(8,128)(2,1)} %bitcast.8) | data formatting | bytes 9175040
  107.6 0.0 copy-done
  107.6 0.0 copy-start.1
  107.6 1.8 %copy.12 = bf16[1,896,2048]{2,1,0:T(8,128)(2,1)} copy(bf16[1,896,2048]{2,1,0:T(8,128)(2,1)S(1)} %bitcast.9) | data formatting | bytes 7340032
  109.4 0.0 copy-done.1
  109.4 0.6 copy.13
Async XLA Ops:
  102.6 5.0 %copy-start = (bf16[896,2048]{1,0:T(8,128)(2,1)S(1)}, bf16[896,2048]{1,0:T(8,128)(2,1)}, u32[]{:S(2)}) copy-start(bf16[896,2048]{1,0:T(8,128)(2,1)} %get-tuple-element.13) | copy-start | bytes 11010052
  107.6 1.8 %copy-start.1 = (f32[2,128]{1,0:T(2,128)S(1)}, f32[2,128]{1,0:T(2,128)}, u32[]{:S(2)}) copy-start(f32[2,128]{1,0:T(2,128)} %get-tuple-element.14) | copy-start | bytes 3076
